TPU v7x, 512 devices: a whole 4x8x8 slice. The times are simulated.
512 devices in a mesh: band: 4 (over x), tile: 16 (over y_lo, z), slab: 8 (over y_hi, core).
Axes of the slice: x: 4, y: 8 (y_hi: 4, y_lo: 2; y = y_hi * 2 + y_lo), z: 8, core: 2. Of those that a mesh axis runs over, the one named last changes fastest.
Arguments:
- strength: float32 [32], P('band'), may hold values from 0.0005 to 0.5
- opacity: float32 [64, 256, 256], P('slab', 'tile'), may hold values from 0.5 to 2
- planck: float32 [64, 256, 256], P('slab', 'tile'), may hold values from 0.5 to 2
- old_populations: float32 [5, 64, 256, 256], P(None, 'slab', 'tile'), may hold values from 0.1 to 1
- line_index: int32 [32], P('band'), may hold values from 0 to 4
- line_weight: float32 [32], P('band'), may hold values from 0.2 to 1
Outputs:
- new_populations: float32 [5, 64, 256, 256], P(None, 'slab', 'tile', 'band')
- new_source: float32 [32, 64, 256, 256], P('band', 'slab', 'tile')
Inputs may be any that keep to these rules, and one draw needn't show every extreme that they name: line_index names a transition of the model atom.
All inputs are finite; a program needn't handle non-finite values.
Results may differ from a plain program's by a relative error of at most 0.0001.
Values sent between devices are 32-bit elements; how exact they have to be, the bound alone decides.
No kernel may reach another device: no remote copies, remote signals or barrier semaphores. Data moves between devices by JAX's collectives and lax.ppermute only.
A program may use at most 64 MiB of HBM per device.

v0:
```python
import jax
import jax.numpy as jnp
from jax import lax
from jax.sharding import PartitionSpec as P

LINES = 5
EPS_THERMAL = 0.1
COLLISION = 0.5
PATH_FACTOR = 1.25
TILT_SHARE = 0.4
LOWER_LEVEL = (0, 0, 1, 1, 2)
UPPER_LEVEL = (3, 4, 3, 4, 4)


def extended_2(cells, sides, width):
    for axis, dim in sides:
        count = lax.axis_size(axis)
        ends = count - 1
        head = lax.slice_in_dim(cells, 0, width, axis=dim)
        tail = lax.slice_in_dim(cells, cells.shape[dim] - width, cells.shape[dim], axis=dim)
        cells = jnp.concatenate(
            [
                lax.ppermute(tail, axis, [(i, (i + 1) % count) for i in range(ends)]),
                cells,
                lax.ppermute(head, axis, [((i + 1) % count, i) for i in range(ends)]),
            ],
            axis=dim,
        )
    return cells


def shifted(block, axis, distance):
    devices = range(lax.axis_size(axis))
    route = [(i - distance, i) for i in devices if i - distance in devices]
    return lax.ppermute(block, axis, route)


def relax(jbar, planck):
    ratios = (jbar + COLLISION * planck[None]) / (1.0 + jbar + COLLISION)
    ground = jnp.ones_like(planck)
    level_three = ratios[0]
    level_four = ratios[1]
    level_one = 0.5 * (level_three / ratios[2] + level_four / ratios[3])
    level_two = level_four / ratios[4]
    stacked = jnp.stack([ground, level_one, level_two, level_three, level_four], axis=0)
    return stacked / jnp.sum(stacked, axis=0)


def line_sources(levels_now):
    return jnp.stack(
        [
            levels_now[UPPER_LEVEL[t]] / (levels_now[LOWER_LEVEL[t]] + levels_now[UPPER_LEVEL[t]])
            for t in range(5)
        ],
        axis=0,
    )


def sweep(face_ext, strength, opacity_ext, source_ext, margin):
    intensity = face_ext
    layer_sums = []
    for plane in range(opacity_ext.shape[0]):
        attenuation = jnp.exp(-PATH_FACTOR * strength[:, None, None] * opacity_ext[plane][None])[
            :, None
        ]
        zero_column = jnp.zeros_like(intensity[:, 0, :1])
        from_left = jnp.concatenate([zero_column, intensity[:, 0, :-1]], axis=1)
        from_right = jnp.concatenate([intensity[:, 1, 1:], zero_column], axis=1)
        upwind = jnp.stack([from_left, from_right], axis=1)
        intensity = (
            attenuation * ((1.0 - TILT_SHARE) * intensity + TILT_SHARE * upwind)
            + (1.0 - attenuation) * source_ext[:, plane][:, None]
        )
        layer_sums.append(jnp.sum(intensity[:, :, margin:-margin], axis=1))
    return (intensity[:, :, margin:-margin], jnp.stack(layer_sums, axis=1))


def per_device(strength, opacity, planck, old_populations, line_index, line_weight):
    highest = lax.Precision.HIGHEST
    slab_depth, tile_rows, cells_y = opacity.shape
    freq_count = strength.shape[0]
    total_freqs = freq_count * lax.axis_size("band")
    onehot = (line_index[:, None] == jnp.arange(LINES, dtype=jnp.int32)[None, :]).astype(
        jnp.float32
    )
    weighted = onehot * line_weight[:, None] * (LINES / (2.0 * total_freqs))
    fields = jnp.concatenate([opacity[None], planck[None], old_populations], axis=0)
    fields_ext = extended_2(fields, (("tile", 2),), slab_depth)
    opacity_ext = fields_ext[0]
    planck_ext = fields_ext[1]
    levels_ext = fields_ext[2:]
    extended = tile_rows + 2 * slab_depth
    global_x = (
        lax.axis_index("tile") * tile_rows - slab_depth + jnp.arange(extended, dtype=jnp.int32)
    )
    inside = ((global_x >= 0) & (global_x < tile_rows * lax.axis_size("tile")))[None, :, None]
    lower_ext = jnp.stack([levels_ext[LOWER_LEVEL[t]] for t in range(5)], axis=0)
    upper_ext = jnp.stack([levels_ext[UPPER_LEVEL[t]] for t in range(5)], axis=0)
    denominator = jnp.where(inside, lower_ext + upper_ext, 1.0)
    line_ext = jnp.where(inside, upper_ext / denominator, 0.0)
    source_ext = jnp.where(
        inside,
        EPS_THERMAL * planck_ext[None]
        + (1.0 - EPS_THERMAL) * jnp.einsum("ft,tzxy->fzxy", onehot, line_ext, precision=highest),
        0.0,
    )
    slab_count = lax.axis_size("slab")

    def whole_step(step, carry):
        face_in, previous = carry
        face_ext = extended_2(face_in, (("tile", 2),), slab_depth)
        bottom, layer_sums = sweep(face_ext, strength, opacity_ext, source_ext, slab_depth)
        return (shifted(bottom, "slab", 1), layer_sums)

    face_start = jnp.zeros((freq_count, 2, tile_rows, cells_y), jnp.float32)
    initial = (face_start, jnp.zeros((freq_count, slab_depth, tile_rows, cells_y), jnp.float32))
    _, layer_sums = lax.fori_loop(0, slab_count, whole_step, initial)
    jbar = jnp.einsum("ft,fzxy->tzxy", weighted, layer_sums, precision=highest)
    share = cells_y // lax.axis_size("band")
    offset = lax.axis_index("band") * share
    jbar_share = lax.psum_scatter(jbar, "band", scatter_dimension=3, tiled=True)
    planck_share = lax.dynamic_slice_in_dim(planck, offset, share, 2)
    populations_share = relax(jbar_share, planck_share)
    populations_all = lax.all_gather(populations_share, "band", axis=3, tiled=True)
    new_source = EPS_THERMAL * planck[None] + (1.0 - EPS_THERMAL) * jnp.einsum(
        "ft,tzxy->fzxy", onehot, line_sources(populations_all), precision=highest
    )
    return (populations_share, new_source)


def solution(mesh):
    in_specs = (
        P("band"),
        P("slab", "tile", None),
        P("slab", "tile", None),
        P(None, "slab", "tile", None),
        P("band"),
        P("band"),
    )
    out_specs = (P(None, "slab", "tile", "band"), P("band", "slab", "tile", None))
    return jax.shard_map(
        per_device, mesh=mesh, in_specs=in_specs, out_specs=out_specs, check_vma=False
    )
```

profile of v0, /device:TPU:8, one launch (start us, length us, event | category | flops | bytes accessed | tf_op | source)
XLA Modules:
  0.0 435.0 jit_solution(6454355539191148617)
XLA Ops:
  8.7 4.3 collective-permute-start.3
  13.0 8.5 %collective-permute-start.4 = (f32[7,8,8,256]{3,2,1,0:T(8,128)S(1)}, f32[7,8,8,256]{3,2,1,0:T(8,128)}, u32[]{:S(2)}, u32[]{:S(2)}) collective-permute-start(f32[7,8,8,256]{3,2,1,0:T(8,128)S(1)} %get-tuple-element.113), channel_id=1, source_target_pairs={{8,0},{16,8},{24,16},{32,24},{40,32},{48,40},{56,48},{64,56},{72,6... | collective-permute-start | bytes 1376264 | tf_op jit(solution)/shard_map/ppermute | solution.py:25
  21.5 8.5 %collective-permute-done.3 = f32[7,8,8,256]{3,2,1,0:T(8,128)S(1)} collective-permute-done((f32[7,8,8,256]{3,2,1,0:T(8,128)S(1)}, f32[7,8,8,256]{3,2,1,0:T(8,128)S(1)}, u32[]{:S(2)}, u32[]{:S(2)}) %collective-permute-start.3) | collective-permute-done | bytes 458784 | tf_op jit(solution)/shard_map/ppermute | solution.py:23
  37.6 251.7 %while.12 = (s32[]{:T(128)}, f32[8,2,16,256]{3,2,0,1:T(8,128)S(1)}, f32[8,8,16,256]{3,2,0,1:T(8,128)}, f32[8]{0:T(128)S(1)}, f32[8,32,256]{2,1,0:T(8,128)S(1)}, /*index=5*/f32[8,8,32,256]{3,2,0,1:T(8,128)}, s32[]{:T(128)}) while((s32[]{:T(128)}, f32[8,2,16,256]{3,2,0,1:T(8,128)S(1)}, f32[8,8,16,256]{3,2,0,1:T(8,128)}, f32[8]{0:T(128)S(1)}, ...), condition=%wide.region_9.10_spmd, body=%wide.region_0.9_spmd.sunk | while | flops 24772616 | bytes 81658408 | solution.py:117
  40.5 6.6 %collective-permute-start.1 = (f32[8,2,8,256]{3,2,0,1:T(8,128)}, f32[8,2,8,256]{3,2,0,1:T(8,128)}, u32[]{:S(2)}, u32[]{:S(2)}) collective-permute-start(f32[8,2,8,256]{3,2,0,1:T(8,128)} %get-tuple-element.218), channel_id=1, source_target_pairs={{8,0},{16,8},{24,16},{32,24},{40,32},{48,40},{56,48},{64,56},{72,6... | collective-permute-start | bytes 393224 | tf_op jit(solution)/shard_map/while/body/eval_jaxpr/ppermute | solution.py:25
  47.2 2.8 multiply_bitcast_fusion.9
  67.0 6.0 %collective-permute-start.1 = (f32[8,2,8,256]{3,2,0,1:T(8,128)}, f32[8,2,8,256]{3,2,0,1:T(8,128)}, u32[]{:S(2)}, u32[]{:S(2)}) collective-permute-start(f32[8,2,8,256]{3,2,0,1:T(8,128)} %get-tuple-element.218), channel_id=1, source_target_pairs={{8,0},{16,8},{24,16},{32,24},{40,32},{48,40},{56,48},{64,56},{72,6... | collective-permute-start | bytes 393224 | tf_op jit(solution)/shard_map/while/body/eval_jaxpr/ppermute | solution.py:25
  73.1 2.8 multiply_bitcast_fusion.9
  87.8 6.8 %collective-permute-start.2 = (f32[8,2,16,256]{3,2,0,1:T(8,128)S(1)}, f32[8,2,16,256]{3,2,0,1:T(8,128)S(1)}, u32[]{:S(2)}, u32[]{:S(2)}) collective-permute-start(f32[8,2,16,256]{3,2,0,1:T(8,128)S(1)} %get-tuple-element.252), channel_id=1, source_target_pairs={{0,1},{1,2},{2,3},{3,4},{4,5},{5,6},{6,7},{8,9},{9,10},{10,11},{11... | collective-permute-start | bytes 786440 | tf_op jit(solution)/shard_map/while/body/eval_jaxpr/ppermute | solution.py:35
  98.5 6.0 %collective-permute-start.1 = (f32[8,2,8,256]{3,2,0,1:T(8,128)}, f32[8,2,8,256]{3,2,0,1:T(8,128)}, u32[]{:S(2)}, u32[]{:S(2)}) collective-permute-start(f32[8,2,8,256]{3,2,0,1:T(8,128)} %get-tuple-element.218), channel_id=1, source_target_pairs={{8,0},{16,8},{24,16},{32,24},{40,32},{48,40},{56,48},{64,56},{72,6... | collective-permute-start | bytes 393224 | tf_op jit(solution)/shard_map/while/body/eval_jaxpr/ppermute | solution.py:25
  104.6 2.8 multiply_bitcast_fusion.9
  119.3 7.5 %collective-permute-start.2 = (f32[8,2,16,256]{3,2,0,1:T(8,128)S(1)}, f32[8,2,16,256]{3,2,0,1:T(8,128)S(1)}, u32[]{:S(2)}, u32[]{:S(2)}) collective-permute-start(f32[8,2,16,256]{3,2,0,1:T(8,128)S(1)} %get-tuple-element.252), channel_id=1, source_target_pairs={{0,1},{1,2},{2,3},{3,4},{4,5},{5,6},{6,7},{8,9},{9,10},{10,11},{11... | collective-permute-start | bytes 786440 | tf_op jit(solution)/shard_map/while/body/eval_jaxpr/ppermute | solution.py:35
  130.7 6.0 %collective-permute-start.1 = (f32[8,2,8,256]{3,2,0,1:T(8,128)}, f32[8,2,8,256]{3,2,0,1:T(8,128)}, u32[]{:S(2)}, u32[]{:S(2)}) collective-permute-start(f32[8,2,8,256]{3,2,0,1:T(8,128)} %get-tuple-element.218), channel_id=1, source_target_pairs={{8,0},{16,8},{24,16},{32,24},{40,32},{48,40},{56,48},{64,56},{72,6... | collective-permute-start | bytes 393224 | tf_op jit(solution)/shard_map/while/body/eval_jaxpr/ppermute | solution.py:25
  136.8 2.8 multiply_bitcast_fusion.9
  151.5 7.6 %collective-permute-start.2 = (f32[8,2,16,256]{3,2,0,1:T(8,128)S(1)}, f32[8,2,16,256]{3,2,0,1:T(8,128)S(1)}, u32[]{:S(2)}, u32[]{:S(2)}) collective-permute-start(f32[8,2,16,256]{3,2,0,1:T(8,128)S(1)} %get-tuple-element.252), channel_id=1, source_target_pairs={{0,1},{1,2},{2,3},{3,4},{4,5},{5,6},{6,7},{8,9},{9,10},{10,11},{11... | collective-permute-start | bytes 786440 | tf_op jit(solution)/shard_map/while/body/eval_jaxpr/ppermute | solution.py:35
  162.9 6.0 %collective-permute-start.1 = (f32[8,2,8,256]{3,2,0,1:T(8,128)}, f32[8,2,8,256]{3,2,0,1:T(8,128)}, u32[]{:S(2)}, u32[]{:S(2)}) collective-permute-start(f32[8,2,8,256]{3,2,0,1:T(8,128)} %get-tuple-element.218), channel_id=1, source_target_pairs={{8,0},{16,8},{24,16},{32,24},{40,32},{48,40},{56,48},{64,56},{72,6... | collective-permute-start | bytes 393224 | tf_op jit(solution)/shard_map/while/body/eval_jaxpr/ppermute | solution.py:25
  169.0 2.8 multiply_bitcast_fusion.9
  183.7 7.6 %collective-permute-start.2 = (f32[8,2,16,256]{3,2,0,1:T(8,128)S(1)}, f32[8,2,16,256]{3,2,0,1:T(8,128)S(1)}, u32[]{:S(2)}, u32[]{:S(2)}) collective-permute-start(f32[8,2,16,256]{3,2,0,1:T(8,128)S(1)} %get-tuple-element.252), channel_id=1, source_target_pairs={{0,1},{1,2},{2,3},{3,4},{4,5},{5,6},{6,7},{8,9},{9,10},{10,11},{11... | collective-permute-start | bytes 786440 | tf_op jit(solution)/shard_map/while/body/eval_jaxpr/ppermute | solution.py:35
  195.1 6.0 %collective-permute-start.1 = (f32[8,2,8,256]{3,2,0,1:T(8,128)}, f32[8,2,8,256]{3,2,0,1:T(8,128)}, u32[]{:S(2)}, u32[]{:S(2)}) collective-permute-start(f32[8,2,8,256]{3,2,0,1:T(8,128)} %get-tuple-element.218), channel_id=1, source_target_pairs={{8,0},{16,8},{24,16},{32,24},{40,32},{48,40},{56,48},{64,56},{72,6... | collective-permute-start | bytes 393224 | tf_op jit(solution)/shard_map/while/body/eval_jaxpr/ppermute | solution.py:25
  201.2 2.8 multiply_bitcast_fusion.9
  215.9 7.6 %collective-permute-start.2 = (f32[8,2,16,256]{3,2,0,1:T(8,128)S(1)}, f32[8,2,16,256]{3,2,0,1:T(8,128)S(1)}, u32[]{:S(2)}, u32[]{:S(2)}) collective-permute-start(f32[8,2,16,256]{3,2,0,1:T(8,128)S(1)} %get-tuple-element.252), channel_id=1, source_target_pairs={{0,1},{1,2},{2,3},{3,4},{4,5},{5,6},{6,7},{8,9},{9,10},{10,11},{11... | collective-permute-start | bytes 786440 | tf_op jit(solution)/shard_map/while/body/eval_jaxpr/ppermute | solution.py:35
  227.3 6.0 %collective-permute-start.1 = (f32[8,2,8,256]{3,2,0,1:T(8,128)}, f32[8,2,8,256]{3,2,0,1:T(8,128)}, u32[]{:S(2)}, u32[]{:S(2)}) collective-permute-start(f32[8,2,8,256]{3,2,0,1:T(8,128)} %get-tuple-element.218), channel_id=1, source_target_pairs={{8,0},{16,8},{24,16},{32,24},{40,32},{48,40},{56,48},{64,56},{72,6... | collective-permute-start | bytes 393224 | tf_op jit(solution)/shard_map/while/body/eval_jaxpr/ppermute | solution.py:25
  248.1 7.6 %collective-permute-start.2 = (f32[8,2,16,256]{3,2,0,1:T(8,128)S(1)}, f32[8,2,16,256]{3,2,0,1:T(8,128)S(1)}, u32[]{:S(2)}, u32[]{:S(2)}) collective-permute-start(f32[8,2,16,256]{3,2,0,1:T(8,128)S(1)} %get-tuple-element.252), channel_id=1, source_target_pairs={{0,1},{1,2},{2,3},{3,4},{4,5},{5,6},{6,7},{8,9},{9,10},{10,11},{11... | collective-permute-start | bytes 786440 | tf_op jit(solution)/shard_map/while/body/eval_jaxpr/ppermute | solution.py:35
  259.5 6.0 %collective-permute-start.1 = (f32[8,2,8,256]{3,2,0,1:T(8,128)}, f32[8,2,8,256]{3,2,0,1:T(8,128)}, u32[]{:S(2)}, u32[]{:S(2)}) collective-permute-start(f32[8,2,8,256]{3,2,0,1:T(8,128)} %get-tuple-element.218), channel_id=1, source_target_pairs={{8,0},{16,8},{24,16},{32,24},{40,32},{48,40},{56,48},{64,56},{72,6... | collective-permute-start | bytes 393224 | tf_op jit(solution)/shard_map/while/body/eval_jaxpr/ppermute | solution.py:25
  280.3 7.8 %collective-permute-start.2 = (f32[8,2,16,256]{3,2,0,1:T(8,128)S(1)}, f32[8,2,16,256]{3,2,0,1:T(8,128)S(1)}, u32[]{:S(2)}, u32[]{:S(2)}) collective-permute-start(f32[8,2,16,256]{3,2,0,1:T(8,128)S(1)} %get-tuple-element.252), channel_id=1, source_target_pairs={{0,1},{1,2},{2,3},{3,4},{4,5},{5,6},{6,7},{8,9},{9,10},{10,11},{11... | collective-permute-start | bytes 786440 | tf_op jit(solution)/shard_map/while/body/eval_jaxpr/ppermute | solution.py:35
  289.3 2.8 fusion.33
  292.1 13.8 %copy.27 = f32[5,8,16,256]{0,2,1,3:T(8,128)} copy(f32[5,8,16,256]{3,0,2,1:T(8,128)S(1)} %fusion.33) | data formatting | bytes 1310720
  305.9 11.9 %reshape.106 = f32[256,640]{1,0:T(8,128)} reshape(f32[256,8,16,5]{3,2,1,0:T(8,128)} %bitcast.211) | data formatting | bytes 1310720
  318.6 43.0 %reduce-scatter.4.cloned.1.call-done = f32[64,640]{1,0:T(8,128)} async-done(((f32[256,640]{1,0:T(8,128)}), f32[64,640]{1,0:T(8,128)}) %reduce-scatter.4.cloned.1.call-update) | async-done | bytes 163856
  361.5 6.2 %reshape.107 = f32[64,8,16,5]{3,2,1,0:T(8,128)} reshape(f32[64,640]{1,0:T(8,128)} %reduce-scatter.4.cloned.1.call-done) | data formatting | bytes 327680
  367.8 3.8 copy.28
  373.9 45.2 %all_gather.3 = f32[5,8,16,256]{2,1,0,3:T(8,128)S(1)} all-gather(f32[5,8,16,64]{2,1,0,3:T(8,128)S(1)} %copy.14), channel_id=1, replica_groups=mesh['band'=4,'tile'=16,'slab'=8] {'band'}, dimensions={3}, use_global_device_ids=true | all-gather | bytes 819200 | tf_op jit(solution)/shard_map/all_gather | solution.py:124
  (646 shorter events, 151.2 us)
Async XLA Ops:
  7.2 354.4 %reduce-scatter.4.cloned.1.call-start = ((), (), s32[]{:S(2)}) async-start(), calls=%async_computation.1 | async-start | bytes 819200
  7.2 24.0 %copy-start.7 = (f32[5,8,16,256]{3,2,1,0:T(8,128)S(1)}, f32[5,8,16,256]{3,2,1,0:T(8,128)}, u32[]{:S(2)}) copy-start(f32[5,8,16,256]{3,2,1,0:T(8,128)} %param.11) | copy-start | bytes 1966084
  7.2 24.0 %copy-start.8 = (f32[8,16,256]{2,1,0:T(8,128)S(1)}, f32[8,16,256]{2,1,0:T(8,128)}, u32[]{:S(2)}) copy-start(f32[8,16,256]{2,1,0:T(8,128)} %param.10) | copy-start | bytes 393220
  7.2 24.0 %copy-start.11 = (f32[8,16,256]{2,1,0:T(8,128)S(1)}, f32[8,16,256]{2,1,0:T(8,128)}, u32[]{:S(2)}) copy-start(f32[8,16,256]{2,1,0:T(8,128)} %param.9) | copy-start | bytes 393220
  8.7 21.3 %collective-permute-start.3 = (f32[7,8,8,256]{3,2,1,0:T(8,128)S(1)}, f32[7,8,8,256]{3,2,1,0:T(8,128)S(1)}, u32[]{:S(2)}, u32[]{:S(2)}) collective-permute-start(f32[7,8,8,256]{3,2,1,0:T(8,128)S(1)} %get-tuple-element.112), channel_id=1, source_target_pairs={{0,8},{8,16},{16,24},{24,32},{32,40},{40,48},{48,56},{56,64},{64,7... | collective-permute-start | bytes 1376264 | tf_op jit(solution)/shard_map/ppermute | solution.py:23
  13.0 18.2 %collective-permute-start.4 = (f32[7,8,8,256]{3,2,1,0:T(8,128)S(1)}, f32[7,8,8,256]{3,2,1,0:T(8,128)}, u32[]{:S(2)}, u32[]{:S(2)}) collective-permute-start(f32[7,8,8,256]{3,2,1,0:T(8,128)S(1)} %get-tuple-element.113), channel_id=1, source_target_pairs={{8,0},{16,8},{24,16},{32,24},{40,32},{48,40},{56,48},{64,56},{72,6... | collective-permute-start | bytes 1376264 | tf_op jit(solution)/shard_map/ppermute | solution.py:25
  37.5 251.7 %copy-start.15 = (f32[8]{0:T(128)S(1)}, f32[8]{0:T(128)}, u32[]{:S(2)}) copy-start(f32[8]{0:T(128)} %param.13) | copy-start | bytes 100
  38.6 13.2 %collective-permute-start = (f32[8,2,8,256]{3,2,0,1:T(8,128)}, f32[8,2,8,256]{3,2,0,1:T(8,128)}, u32[]{:S(2)}, u32[]{:S(2)}) collective-permute-start(f32[8,2,8,256]{3,2,0,1:T(8,128)} %get-tuple-element.217), channel_id=1, source_target_pairs={{0,8},{8,16},{16,24},{24,32},{32,40},{40,48},{48,56},{56,64},{64,7... | collective-permute-start | bytes 393224 | tf_op jit(solution)/shard_map/while/body/eval_jaxpr/ppermute | solution.py:23
  40.5 13.1 %collective-permute-start.1 = (f32[8,2,8,256]{3,2,0,1:T(8,128)}, f32[8,2,8,256]{3,2,0,1:T(8,128)}, u32[]{:S(2)}, u32[]{:S(2)}) collective-permute-start(f32[8,2,8,256]{3,2,0,1:T(8,128)} %get-tuple-element.218), channel_id=1, source_target_pairs={{8,0},{16,8},{24,16},{32,24},{40,32},{48,40},{56,48},{64,56},{72,6... | collective-permute-start | bytes 393224 | tf_op jit(solution)/shard_map/while/body/eval_jaxpr/ppermute | solution.py:25
  61.9 2.4 collective-permute-start.2
  65.1 12.6 %collective-permute-start = (f32[8,2,8,256]{3,2,0,1:T(8,128)}, f32[8,2,8,256]{3,2,0,1:T(8,128)}, u32[]{:S(2)}, u32[]{:S(2)}) collective-permute-start(f32[8,2,8,256]{3,2,0,1:T(8,128)} %get-tuple-element.217), channel_id=1, source_target_pairs={{0,8},{8,16},{16,24},{24,32},{32,40},{40,48},{48,56},{56,64},{64,7... | collective-permute-start | bytes 393224 | tf_op jit(solution)/shard_map/while/body/eval_jaxpr/ppermute | solution.py:23
  67.0 12.6 %collective-permute-start.1 = (f32[8,2,8,256]{3,2,0,1:T(8,128)}, f32[8,2,8,256]{3,2,0,1:T(8,128)}, u32[]{:S(2)}, u32[]{:S(2)}) collective-permute-start(f32[8,2,8,256]{3,2,0,1:T(8,128)} %get-tuple-element.218), channel_id=1, source_target_pairs={{8,0},{16,8},{24,16},{32,24},{40,32},{48,40},{56,48},{64,56},{72,6... | collective-permute-start | bytes 393224 | tf_op jit(solution)/shard_map/while/body/eval_jaxpr/ppermute | solution.py:25
  87.8 8.0 %collective-permute-start.2 = (f32[8,2,16,256]{3,2,0,1:T(8,128)S(1)}, f32[8,2,16,256]{3,2,0,1:T(8,128)S(1)}, u32[]{:S(2)}, u32[]{:S(2)}) collective-permute-start(f32[8,2,16,256]{3,2,0,1:T(8,128)S(1)} %get-tuple-element.252), channel_id=1, source_target_pairs={{0,1},{1,2},{2,3},{3,4},{4,5},{5,6},{6,7},{8,9},{9,10},{10,11},{11... | collective-permute-start | bytes 786440 | tf_op jit(solution)/shard_map/while/body/eval_jaxpr/ppermute | solution.py:35
  96.6 12.6 %collective-permute-start = (f32[8,2,8,256]{3,2,0,1:T(8,128)}, f32[8,2,8,256]{3,2,0,1:T(8,128)}, u32[]{:S(2)}, u32[]{:S(2)}) collective-permute-start(f32[8,2,8,256]{3,2,0,1:T(8,128)} %get-tuple-element.217), channel_id=1, source_target_pairs={{0,8},{8,16},{16,24},{24,32},{32,40},{40,48},{48,56},{56,64},{64,7... | collective-permute-start | bytes 393224 | tf_op jit(solution)/shard_map/while/body/eval_jaxpr/ppermute | solution.py:23
  98.5 12.6 %collective-permute-start.1 = (f32[8,2,8,256]{3,2,0,1:T(8,128)}, f32[8,2,8,256]{3,2,0,1:T(8,128)}, u32[]{:S(2)}, u32[]{:S(2)}) collective-permute-start(f32[8,2,8,256]{3,2,0,1:T(8,128)} %get-tuple-element.218), channel_id=1, source_target_pairs={{8,0},{16,8},{24,16},{32,24},{40,32},{48,40},{56,48},{64,56},{72,6... | collective-permute-start | bytes 393224 | tf_op jit(solution)/shard_map/while/body/eval_jaxpr/ppermute | solution.py:25
  119.3 8.6 %collective-permute-start.2 = (f32[8,2,16,256]{3,2,0,1:T(8,128)S(1)}, f32[8,2,16,256]{3,2,0,1:T(8,128)S(1)}, u32[]{:S(2)}, u32[]{:S(2)}) collective-permute-start(f32[8,2,16,256]{3,2,0,1:T(8,128)S(1)} %get-tuple-element.252), channel_id=1, source_target_pairs={{0,1},{1,2},{2,3},{3,4},{4,5},{5,6},{6,7},{8,9},{9,10},{10,11},{11... | collective-permute-start | bytes 786440 | tf_op jit(solution)/shard_map/while/body/eval_jaxpr/ppermute | solution.py:35
  128.7 12.6 %collective-permute-start = (f32[8,2,8,256]{3,2,0,1:T(8,128)}, f32[8,2,8,256]{3,2,0,1:T(8,128)}, u32[]{:S(2)}, u32[]{:S(2)}) collective-permute-start(f32[8,2,8,256]{3,2,0,1:T(8,128)} %get-tuple-element.217), channel_id=1, source_target_pairs={{0,8},{8,16},{16,24},{24,32},{32,40},{40,48},{48,56},{56,64},{64,7... | collective-permute-start | bytes 393224 | tf_op jit(solution)/shard_map/while/body/eval_jaxpr/ppermute | solution.py:23
  130.7 12.6 %collective-permute-start.1 = (f32[8,2,8,256]{3,2,0,1:T(8,128)}, f32[8,2,8,256]{3,2,0,1:T(8,128)}, u32[]{:S(2)}, u32[]{:S(2)}) collective-permute-start(f32[8,2,8,256]{3,2,0,1:T(8,128)} %get-tuple-element.218), channel_id=1, source_target_pairs={{8,0},{16,8},{24,16},{32,24},{40,32},{48,40},{56,48},{64,56},{72,6... | collective-permute-start | bytes 393224 | tf_op jit(solution)/shard_map/while/body/eval_jaxpr/ppermute | solution.py:25
  151.5 8.7 %collective-permute-start.2 = (f32[8,2,16,256]{3,2,0,1:T(8,128)S(1)}, f32[8,2,16,256]{3,2,0,1:T(8,128)S(1)}, u32[]{:S(2)}, u32[]{:S(2)}) collective-permute-start(f32[8,2,16,256]{3,2,0,1:T(8,128)S(1)} %get-tuple-element.252), channel_id=1, source_target_pairs={{0,1},{1,2},{2,3},{3,4},{4,5},{5,6},{6,7},{8,9},{9,10},{10,11},{11... | collective-permute-start | bytes 786440 | tf_op jit(solution)/shard_map/while/body/eval_jaxpr/ppermute | solution.py:35
  160.9 12.6 %collective-permute-start = (f32[8,2,8,256]{3,2,0,1:T(8,128)}, f32[8,2,8,256]{3,2,0,1:T(8,128)}, u32[]{:S(2)}, u32[]{:S(2)}) collective-permute-start(f32[8,2,8,256]{3,2,0,1:T(8,128)} %get-tuple-element.217), channel_id=1, source_target_pairs={{0,8},{8,16},{16,24},{24,32},{32,40},{40,48},{48,56},{56,64},{64,7... | collective-permute-start | bytes 393224 | tf_op jit(solution)/shard_map/while/body/eval_jaxpr/ppermute | solution.py:23
  162.9 12.6 %collective-permute-start.1 = (f32[8,2,8,256]{3,2,0,1:T(8,128)}, f32[8,2,8,256]{3,2,0,1:T(8,128)}, u32[]{:S(2)}, u32[]{:S(2)}) collective-permute-start(f32[8,2,8,256]{3,2,0,1:T(8,128)} %get-tuple-element.218), channel_id=1, source_target_pairs={{8,0},{16,8},{24,16},{32,24},{40,32},{48,40},{56,48},{64,56},{72,6... | collective-permute-start | bytes 393224 | tf_op jit(solution)/shard_map/while/body/eval_jaxpr/ppermute | solution.py:25
  183.7 8.7 %collective-permute-start.2 = (f32[8,2,16,256]{3,2,0,1:T(8,128)S(1)}, f32[8,2,16,256]{3,2,0,1:T(8,128)S(1)}, u32[]{:S(2)}, u32[]{:S(2)}) collective-permute-start(f32[8,2,16,256]{3,2,0,1:T(8,128)S(1)} %get-tuple-element.252), channel_id=1, source_target_pairs={{0,1},{1,2},{2,3},{3,4},{4,5},{5,6},{6,7},{8,9},{9,10},{10,11},{11... | collective-permute-start | bytes 786440 | tf_op jit(solution)/shard_map/while/body/eval_jaxpr/ppermute | solution.py:35
  193.2 12.6 %collective-permute-start = (f32[8,2,8,256]{3,2,0,1:T(8,128)}, f32[8,2,8,256]{3,2,0,1:T(8,128)}, u32[]{:S(2)}, u32[]{:S(2)}) collective-permute-start(f32[8,2,8,256]{3,2,0,1:T(8,128)} %get-tuple-element.217), channel_id=1, source_target_pairs={{0,8},{8,16},{16,24},{24,32},{32,40},{40,48},{48,56},{56,64},{64,7... | collective-permute-start | bytes 393224 | tf_op jit(solution)/shard_map/while/body/eval_jaxpr/ppermute | solution.py:23
  195.1 12.6 %collective-permute-start.1 = (f32[8,2,8,256]{3,2,0,1:T(8,128)}, f32[8,2,8,256]{3,2,0,1:T(8,128)}, u32[]{:S(2)}, u32[]{:S(2)}) collective-permute-start(f32[8,2,8,256]{3,2,0,1:T(8,128)} %get-tuple-element.218), channel_id=1, source_target_pairs={{8,0},{16,8},{24,16},{32,24},{40,32},{48,40},{56,48},{64,56},{72,6... | collective-permute-start | bytes 393224 | tf_op jit(solution)/shard_map/while/body/eval_jaxpr/ppermute | solution.py:25
  215.9 8.7 %collective-permute-start.2 = (f32[8,2,16,256]{3,2,0,1:T(8,128)S(1)}, f32[8,2,16,256]{3,2,0,1:T(8,128)S(1)}, u32[]{:S(2)}, u32[]{:S(2)}) collective-permute-start(f32[8,2,16,256]{3,2,0,1:T(8,128)S(1)} %get-tuple-element.252), channel_id=1, source_target_pairs={{0,1},{1,2},{2,3},{3,4},{4,5},{5,6},{6,7},{8,9},{9,10},{10,11},{11... | collective-permute-start | bytes 786440 | tf_op jit(solution)/shard_map/while/body/eval_jaxpr/ppermute | solution.py:35
  225.4 12.6 %collective-permute-start = (f32[8,2,8,256]{3,2,0,1:T(8,128)}, f32[8,2,8,256]{3,2,0,1:T(8,128)}, u32[]{:S(2)}, u32[]{:S(2)}) collective-permute-start(f32[8,2,8,256]{3,2,0,1:T(8,128)} %get-tuple-element.217), channel_id=1, source_target_pairs={{0,8},{8,16},{16,24},{24,32},{32,40},{40,48},{48,56},{56,64},{64,7... | collective-permute-start | bytes 393224 | tf_op jit(solution)/shard_map/while/body/eval_jaxpr/ppermute | solution.py:23
  227.3 12.6 %collective-permute-start.1 = (f32[8,2,8,256]{3,2,0,1:T(8,128)}, f32[8,2,8,256]{3,2,0,1:T(8,128)}, u32[]{:S(2)}, u32[]{:S(2)}) collective-permute-start(f32[8,2,8,256]{3,2,0,1:T(8,128)} %get-tuple-element.218), channel_id=1, source_target_pairs={{8,0},{16,8},{24,16},{32,24},{40,32},{48,40},{56,48},{64,56},{72,6... | collective-permute-start | bytes 393224 | tf_op jit(solution)/shard_map/while/body/eval_jaxpr/ppermute | solution.py:25
  248.1 8.7 %collective-permute-start.2 = (f32[8,2,16,256]{3,2,0,1:T(8,128)S(1)}, f32[8,2,16,256]{3,2,0,1:T(8,128)S(1)}, u32[]{:S(2)}, u32[]{:S(2)}) collective-permute-start(f32[8,2,16,256]{3,2,0,1:T(8,128)S(1)} %get-tuple-element.252), channel_id=1, source_target_pairs={{0,1},{1,2},{2,3},{3,4},{4,5},{5,6},{6,7},{8,9},{9,10},{10,11},{11... | collective-permute-start | bytes 786440 | tf_op jit(solution)/shard_map/while/body/eval_jaxpr/ppermute | solution.py:35
  257.6 12.6 %collective-permute-start = (f32[8,2,8,256]{3,2,0,1:T(8,128)}, f32[8,2,8,256]{3,2,0,1:T(8,128)}, u32[]{:S(2)}, u32[]{:S(2)}) collective-permute-start(f32[8,2,8,256]{3,2,0,1:T(8,128)} %get-tuple-element.217), channel_id=1, source_target_pairs={{0,8},{8,16},{16,24},{24,32},{32,40},{40,48},{48,56},{56,64},{64,7... | collective-permute-start | bytes 393224 | tf_op jit(solution)/shard_map/while/body/eval_jaxpr/ppermute | solution.py:23
  259.5 12.6 %collective-permute-start.1 = (f32[8,2,8,256]{3,2,0,1:T(8,128)}, f32[8,2,8,256]{3,2,0,1:T(8,128)}, u32[]{:S(2)}, u32[]{:S(2)}) collective-permute-start(f32[8,2,8,256]{3,2,0,1:T(8,128)} %get-tuple-element.218), channel_id=1, source_target_pairs={{8,0},{16,8},{24,16},{32,24},{40,32},{48,40},{56,48},{64,56},{72,6... | collective-permute-start | bytes 393224 | tf_op jit(solution)/shard_map/while/body/eval_jaxpr/ppermute | solution.py:25
  280.3 9.0 %collective-permute-start.2 = (f32[8,2,16,256]{3,2,0,1:T(8,128)S(1)}, f32[8,2,16,256]{3,2,0,1:T(8,128)S(1)}, u32[]{:S(2)}, u32[]{:S(2)}) collective-permute-start(f32[8,2,16,256]{3,2,0,1:T(8,128)S(1)} %get-tuple-element.252), channel_id=1, source_target_pairs={{0,1},{1,2},{2,3},{3,4},{4,5},{5,6},{6,7},{8,9},{9,10},{10,11},{11... | collective-permute-start | bytes 786440 | tf_op jit(solution)/shard_map/while/body/eval_jaxpr/ppermute | solution.py:35
  305.9 11.9 %copy-start.9 = (f32[8,16,256]{2,1,0:T(8,128)S(1)}, f32[8,16,256]{2,1,0:T(8,128)}, u32[]{:S(2)}) copy-start(f32[8,16,256]{2,1,0:T(8,128)} %param.10) | copy-start | bytes 393220
  (68 other events, 249.1 us)
Sparse Core Ops, SparseCore 0:
  317.9 43.5 reduce-scatter.3
where the time goes:
time: 438 us; the launch traced here: 435 us
  starting transfers between devices  131 us (30%)
  local copies, waits for them, and re-layouts  107 us (24%)
  other arithmetic  69.3 us (16%)
  waiting for transfers between devices  59.8 us (14%)
  blocking collectives  45.2 us (10%)
  between operations  14.3 us (3%)
  matrix products  5.26 us (1%)
    ppermute x9, starting transfers between devices, extended_2(): lax.ppermute(head, axis, [((i + 1) % count, i) for i in range(ends)])  57.3 us
    ppermute x8, starting transfers between devices, shifted(): return lax.ppermute(block, axis, route)  53.7 us
    add x64, other arithmetic, sweep(): attenuation * ((1.0 - TILT_SHARE) * intensity + TILT_SHARE * upwind)  51.4 us
    all_gather x1, blocking collectives, per_device(): lax.all_gather(populations_share, 'band', axis=3, tiled=True)  45.2 us
    unnamed x29, local copies, waits for them, and re-layouts  43.1 us
    unnamed x2, waiting for transfers between devices  43 us
    while x200, local copies, waits for them, and re-layouts  35.4 us
    ppermute x9, starting transfers between devices, extended_2(): lax.ppermute(tail, axis, [(i, (i + 1) % count) for i in range(ends)])  19.6 us
  transfers between devices with their start and end apart: 27, of which 11 were waited for; matrix products, arithmetic and copies ran while one was open for 12% of the time, Pallas kernels for 0%

commit v1 on v0

--- a/solution.py
+++ b/solution.py
@@ -10,6 +10,19 @@
 TILT_SHARE = 0.4
 LOWER_LEVEL = (0, 0, 1, 1, 2)
 UPPER_LEVEL = (3, 4, 3, 4, 4)
+
+
+def collect(shard, axis, dim):
+    ways = lax.axis_size(axis)
+    up = [(d, (d + 1) % ways) for d in range(ways)]
+    down = [(d, (d - 1) % ways) for d in range(ways)]
+    earlier, later = ([shard], [shard])
+    for _ in range(ways // 2):
+        earlier.append(lax.ppermute(earlier[-1], axis, up))
+    for _ in range((ways - 1) // 2):
+        later.append(lax.ppermute(later[-1], axis, down))
+    line = jnp.concatenate([*earlier[::-1], *later[1:]], axis=dim)
+    return jnp.roll(line, (lax.axis_index(axis) - ways // 2) * shard.shape[dim], axis=dim)
 
 
 def extended_2(cells, sides, width):
@@ -121,7 +134,7 @@
     jbar_share = lax.psum_scatter(jbar, "band", scatter_dimension=3, tiled=True)
     planck_share = lax.dynamic_slice_in_dim(planck, offset, share, 2)
     populations_share = relax(jbar_share, planck_share)
-    populations_all = lax.all_gather(populations_share, "band", axis=3, tiled=True)
+    populations_all = collect(populations_share, "band", 3)
     new_source = EPS_THERMAL * planck[None] + (1.0 - EPS_THERMAL) * jnp.einsum(
         "ft,tzxy->fzxy", onehot, line_sources(populations_all), precision=highest
     )

time: 438 us -> 420 us (0.959)
  blocking collectives: 45.2 us -> 0 us
  waiting for transfers between devices: 59.8 us -> 80.2 us
  starting transfers between devices: 131 us -> 140 us
    all_gather x1 -> x0, blocking collectives: 45.2 us -> none  [per_device(): lax.all_gather(populations_share, 'band', axis=3, tiled=True)]
    ppermute x0 -> x3, waiting for transfers between devices: none -> 19.7 us  [the longest x2 19.7 us: collect(): earlier.append(lax.ppermute(earlier[-1], axis, up))]
    ppermute x0 -> x3, starting transfers between devices: none -> 8.96 us  [the longest x1 5.13 us: collect(): later.append(lax.ppermute(later[-1], axis, down))]
    unnamed x29 -> x24, local copies, waits for them, and re-layouts: 43.1 us -> 39.6 us
  transfers between devices with their start and end apart: 27 -> 30, of which waited for: 11 -> 13; matrix products, arithmetic and copies ran while one was open for 12% -> 13% of each run, Pallas kernels for 0% -> 0%
where the time goes in v1:
time: 420 us; the launch traced here: 418 us
  starting transfers between devices  140 us (33%)
  local copies, waits for them, and re-layouts  104 us (25%)
  waiting for transfers between devices  80.2 us (19%)
  other arithmetic  70 us (17%)
  between operations  14.3 us (3%)
  matrix products  5.26 us (1%)
    ppermute x9, starting transfers between devices, extended_2(): lax.ppermute(head, axis, [((i + 1) % count, i) for i in range(ends)])  57.3 us
    ppermute x8, starting transfers between devices, shifted(): return lax.ppermute(block, axis, route)  53.8 us
    add x64, other arithmetic, sweep(): attenuation * ((1.0 - TILT_SHARE) * intensity + TILT_SHARE * upwind)  51.4 us
    unnamed x2, waiting for transfers between devices  43.7 us
    unnamed x24, local copies, waits for them, and re-layouts  39.6 us
    while x200, local copies, waits for them, and re-layouts  35.4 us
    ppermute x2, waiting for transfers between devices, collect(): earlier.append(lax.ppermute(earlier[-1], axis, up))  19.7 us
    ppermute x9, starting transfers between devices, extended_2(): lax.ppermute(tail, axis, [(i, (i + 1) % count) for i in range(ends)])  19.6 us
  transfers between devices with their start and end apart: 30, of which 13 were waited for; matrix products, arithmetic and copies ran while one was open for 13% of the time, Pallas kernels for 0%

profile of v1, /device:TPU:8, one launch (start us, length us, event | category | flops | bytes accessed | tf_op | source)
XLA Modules:
  0.0 417.7 jit_solution(6495448627549572889)
XLA Ops:
  8.7 4.3 %collective-permute-start.3 = (f32[7,8,8,256]{3,2,1,0:T(8,128)S(1)}, f32[7,8,8,256]{3,2,1,0:T(8,128)S(1)}, u32[]{:S(2)}, u32[]{:S(2)}) collective-permute-start(f32[7,8,8,256]{3,2,1,0:T(8,128)S(1)} %get-tuple-element.112), channel_id=1, source_target_pairs={{0,8},{8,16},{16,24},{24,32},{32,40},{40,48},{48,56},{56,64},{64,7... | collective-permute-start | bytes 1376264 | tf_op jit(solution)/shard_map/ppermute | solution.py:36
  13.0 8.5 %collective-permute-start.4 = (f32[7,8,8,256]{3,2,1,0:T(8,128)S(1)}, f32[7,8,8,256]{3,2,1,0:T(8,128)}, u32[]{:S(2)}, u32[]{:S(2)}) collective-permute-start(f32[7,8,8,256]{3,2,1,0:T(8,128)S(1)} %get-tuple-element.113), channel_id=1, source_target_pairs={{8,0},{16,8},{24,16},{32,24},{40,32},{48,40},{56,48},{64,56},{72,6... | collective-permute-start | bytes 1376264 | tf_op jit(solution)/shard_map/ppermute | solution.py:38
  21.5 8.5 %collective-permute-done.3 = f32[7,8,8,256]{3,2,1,0:T(8,128)S(1)} collective-permute-done((f32[7,8,8,256]{3,2,1,0:T(8,128)S(1)}, f32[7,8,8,256]{3,2,1,0:T(8,128)S(1)}, u32[]{:S(2)}, u32[]{:S(2)}) %collective-permute-start.3) | collective-permute-done | bytes 458784 | tf_op jit(solution)/shard_map/ppermute | solution.py:36
  37.6 252.0 %while.12 = (s32[]{:T(128)}, f32[8,2,16,256]{3,2,0,1:T(8,128)S(1)}, f32[8,8,16,256]{3,2,0,1:T(8,128)}, f32[8]{0:T(128)S(1)}, f32[8,32,256]{2,1,0:T(8,128)S(1)}, /*index=5*/f32[8,8,32,256]{3,2,0,1:T(8,128)}, s32[]{:T(128)}) while((s32[]{:T(128)}, f32[8,2,16,256]{3,2,0,1:T(8,128)S(1)}, f32[8,8,16,256]{3,2,0,1:T(8,128)}, f32[8]{0:T(128)S(1)}, ...), condition=%wide.region_9.10_spmd, body=%wide.region_0.9_spmd.sunk | while | flops 24772616 | bytes 81658408 | solution.py:130
  40.5 6.6 %collective-permute-start.1 = (f32[8,2,8,256]{3,2,0,1:T(8,128)}, f32[8,2,8,256]{3,2,0,1:T(8,128)}, u32[]{:S(2)}, u32[]{:S(2)}) collective-permute-start(f32[8,2,8,256]{3,2,0,1:T(8,128)} %get-tuple-element.208), channel_id=1, source_target_pairs={{8,0},{16,8},{24,16},{32,24},{40,32},{48,40},{56,48},{64,56},{72,6... | collective-permute-start | bytes 393224 | tf_op jit(solution)/shard_map/while/body/eval_jaxpr/ppermute | solution.py:38
  47.2 2.8 multiply_bitcast_fusion.9
  67.1 6.0 %collective-permute-start.1 = (f32[8,2,8,256]{3,2,0,1:T(8,128)}, f32[8,2,8,256]{3,2,0,1:T(8,128)}, u32[]{:S(2)}, u32[]{:S(2)}) collective-permute-start(f32[8,2,8,256]{3,2,0,1:T(8,128)} %get-tuple-element.208), channel_id=1, source_target_pairs={{8,0},{16,8},{24,16},{32,24},{40,32},{48,40},{56,48},{64,56},{72,6... | collective-permute-start | bytes 393224 | tf_op jit(solution)/shard_map/while/body/eval_jaxpr/ppermute | solution.py:38
  73.2 2.8 multiply_bitcast_fusion.9
  87.9 6.8 %collective-permute-start.2 = (f32[8,2,16,256]{3,2,0,1:T(8,128)S(1)}, f32[8,2,16,256]{3,2,0,1:T(8,128)S(1)}, u32[]{:S(2)}, u32[]{:S(2)}) collective-permute-start(f32[8,2,16,256]{3,2,0,1:T(8,128)S(1)} %get-tuple-element.242), channel_id=1, source_target_pairs={{0,1},{1,2},{2,3},{3,4},{4,5},{5,6},{6,7},{8,9},{9,10},{10,11},{11... | collective-permute-start | bytes 786440 | tf_op jit(solution)/shard_map/while/body/eval_jaxpr/ppermute | solution.py:48
  98.6 6.0 %collective-permute-start.1 = (f32[8,2,8,256]{3,2,0,1:T(8,128)}, f32[8,2,8,256]{3,2,0,1:T(8,128)}, u32[]{:S(2)}, u32[]{:S(2)}) collective-permute-start(f32[8,2,8,256]{3,2,0,1:T(8,128)} %get-tuple-element.208), channel_id=1, source_target_pairs={{8,0},{16,8},{24,16},{32,24},{40,32},{48,40},{56,48},{64,56},{72,6... | collective-permute-start | bytes 393224 | tf_op jit(solution)/shard_map/while/body/eval_jaxpr/ppermute | solution.py:38
  119.4 7.5 %collective-permute-start.2 = (f32[8,2,16,256]{3,2,0,1:T(8,128)S(1)}, f32[8,2,16,256]{3,2,0,1:T(8,128)S(1)}, u32[]{:S(2)}, u32[]{:S(2)}) collective-permute-start(f32[8,2,16,256]{3,2,0,1:T(8,128)S(1)} %get-tuple-element.242), channel_id=1, source_target_pairs={{0,1},{1,2},{2,3},{3,4},{4,5},{5,6},{6,7},{8,9},{9,10},{10,11},{11... | collective-permute-start | bytes 786440 | tf_op jit(solution)/shard_map/while/body/eval_jaxpr/ppermute | solution.py:48
  130.7 6.0 %collective-permute-start.1 = (f32[8,2,8,256]{3,2,0,1:T(8,128)}, f32[8,2,8,256]{3,2,0,1:T(8,128)}, u32[]{:S(2)}, u32[]{:S(2)}) collective-permute-start(f32[8,2,8,256]{3,2,0,1:T(8,128)} %get-tuple-element.208), channel_id=1, source_target_pairs={{8,0},{16,8},{24,16},{32,24},{40,32},{48,40},{56,48},{64,56},{72,6... | collective-permute-start | bytes 393224 | tf_op jit(solution)/shard_map/while/body/eval_jaxpr/ppermute | solution.py:38
  151.6 7.6 %collective-permute-start.2 = (f32[8,2,16,256]{3,2,0,1:T(8,128)S(1)}, f32[8,2,16,256]{3,2,0,1:T(8,128)S(1)}, u32[]{:S(2)}, u32[]{:S(2)}) collective-permute-start(f32[8,2,16,256]{3,2,0,1:T(8,128)S(1)} %get-tuple-element.242), channel_id=1, source_target_pairs={{0,1},{1,2},{2,3},{3,4},{4,5},{5,6},{6,7},{8,9},{9,10},{10,11},{11... | collective-permute-start | bytes 786440 | tf_op jit(solution)/shard_map/while/body/eval_jaxpr/ppermute | solution.py:48
  163.0 6.0 %collective-permute-start.1 = (f32[8,2,8,256]{3,2,0,1:T(8,128)}, f32[8,2,8,256]{3,2,0,1:T(8,128)}, u32[]{:S(2)}, u32[]{:S(2)}) collective-permute-start(f32[8,2,8,256]{3,2,0,1:T(8,128)} %get-tuple-element.208), channel_id=1, source_target_pairs={{8,0},{16,8},{24,16},{32,24},{40,32},{48,40},{56,48},{64,56},{72,6... | collective-permute-start | bytes 393224 | tf_op jit(solution)/shard_map/while/body/eval_jaxpr/ppermute | solution.py:38
  183.8 7.6 %collective-permute-start.2 = (f32[8,2,16,256]{3,2,0,1:T(8,128)S(1)}, f32[8,2,16,256]{3,2,0,1:T(8,128)S(1)}, u32[]{:S(2)}, u32[]{:S(2)}) collective-permute-start(f32[8,2,16,256]{3,2,0,1:T(8,128)S(1)} %get-tuple-element.242), channel_id=1, source_target_pairs={{0,1},{1,2},{2,3},{3,4},{4,5},{5,6},{6,7},{8,9},{9,10},{10,11},{11... | collective-permute-start | bytes 786440 | tf_op jit(solution)/shard_map/while/body/eval_jaxpr/ppermute | solution.py:48
  195.2 6.0 %collective-permute-start.1 = (f32[8,2,8,256]{3,2,0,1:T(8,128)}, f32[8,2,8,256]{3,2,0,1:T(8,128)}, u32[]{:S(2)}, u32[]{:S(2)}) collective-permute-start(f32[8,2,8,256]{3,2,0,1:T(8,128)} %get-tuple-element.208), channel_id=1, source_target_pairs={{8,0},{16,8},{24,16},{32,24},{40,32},{48,40},{56,48},{64,56},{72,6... | collective-permute-start | bytes 393224 | tf_op jit(solution)/shard_map/while/body/eval_jaxpr/ppermute | solution.py:38
  216.1 7.6 %collective-permute-start.2 = (f32[8,2,16,256]{3,2,0,1:T(8,128)S(1)}, f32[8,2,16,256]{3,2,0,1:T(8,128)S(1)}, u32[]{:S(2)}, u32[]{:S(2)}) collective-permute-start(f32[8,2,16,256]{3,2,0,1:T(8,128)S(1)} %get-tuple-element.242), channel_id=1, source_target_pairs={{0,1},{1,2},{2,3},{3,4},{4,5},{5,6},{6,7},{8,9},{9,10},{10,11},{11... | collective-permute-start | bytes 786440 | tf_op jit(solution)/shard_map/while/body/eval_jaxpr/ppermute | solution.py:48
  227.5 6.0 %collective-permute-start.1 = (f32[8,2,8,256]{3,2,0,1:T(8,128)}, f32[8,2,8,256]{3,2,0,1:T(8,128)}, u32[]{:S(2)}, u32[]{:S(2)}) collective-permute-start(f32[8,2,8,256]{3,2,0,1:T(8,128)} %get-tuple-element.208), channel_id=1, source_target_pairs={{8,0},{16,8},{24,16},{32,24},{40,32},{48,40},{56,48},{64,56},{72,6... | collective-permute-start | bytes 393224 | tf_op jit(solution)/shard_map/while/body/eval_jaxpr/ppermute | solution.py:38
  233.6 2.8 multiply_bitcast_fusion.9
  248.3 7.6 %collective-permute-start.2 = (f32[8,2,16,256]{3,2,0,1:T(8,128)S(1)}, f32[8,2,16,256]{3,2,0,1:T(8,128)S(1)}, u32[]{:S(2)}, u32[]{:S(2)}) collective-permute-start(f32[8,2,16,256]{3,2,0,1:T(8,128)S(1)} %get-tuple-element.242), channel_id=1, source_target_pairs={{0,1},{1,2},{2,3},{3,4},{4,5},{5,6},{6,7},{8,9},{9,10},{10,11},{11... | collective-permute-start | bytes 786440 | tf_op jit(solution)/shard_map/while/body/eval_jaxpr/ppermute | solution.py:48
  259.7 6.0 %collective-permute-start.1 = (f32[8,2,8,256]{3,2,0,1:T(8,128)}, f32[8,2,8,256]{3,2,0,1:T(8,128)}, u32[]{:S(2)}, u32[]{:S(2)}) collective-permute-start(f32[8,2,8,256]{3,2,0,1:T(8,128)} %get-tuple-element.208), channel_id=1, source_target_pairs={{8,0},{16,8},{24,16},{32,24},{40,32},{48,40},{56,48},{64,56},{72,6... | collective-permute-start | bytes 393224 | tf_op jit(solution)/shard_map/while/body/eval_jaxpr/ppermute | solution.py:38
  280.6 7.8 %collective-permute-start.2 = (f32[8,2,16,256]{3,2,0,1:T(8,128)S(1)}, f32[8,2,16,256]{3,2,0,1:T(8,128)S(1)}, u32[]{:S(2)}, u32[]{:S(2)}) collective-permute-start(f32[8,2,16,256]{3,2,0,1:T(8,128)S(1)} %get-tuple-element.242), channel_id=1, source_target_pairs={{0,1},{1,2},{2,3},{3,4},{4,5},{5,6},{6,7},{8,9},{9,10},{10,11},{11... | collective-permute-start | bytes 786440 | tf_op jit(solution)/shard_map/while/body/eval_jaxpr/ppermute | solution.py:48
  289.6 2.8 fusion.33
  292.3 13.8 %copy.21 = f32[5,8,16,256]{0,2,1,3:T(8,128)} copy(f32[5,8,16,256]{3,0,2,1:T(8,128)S(1)} %fusion.33) | data formatting | bytes 1310720
  306.1 11.9 %reshape.106 = f32[256,640]{1,0:T(8,128)} reshape(f32[256,8,16,5]{3,2,1,0:T(8,128)} %bitcast.201) | data formatting | bytes 1310720
  318.1 43.7 %reduce-scatter.4.cloned.1.call-done = f32[64,640]{1,0:T(8,128)} async-done(((f32[256,640]{1,0:T(8,128)}), f32[64,640]{1,0:T(8,128)}) %reduce-scatter.4.cloned.1.call-update) | async-done | bytes 163856
  361.8 6.2 %reshape.107 = f32[64,8,16,5]{3,2,1,0:T(8,128)} reshape(f32[64,640]{1,0:T(8,128)} %reduce-scatter.4.cloned.1.call-done) | data formatting | bytes 327680
  368.0 3.8 copy.22
  374.8 5.1 %collective-permute-start.7 = (f32[5,8,16,64]{3,0,2,1:T(8,128)S(1)}, f32[5,8,16,64]{3,0,2,1:T(8,128)S(1)}, u32[]{:S(2)}, u32[]{:S(2)}) collective-permute-start(f32[5,8,16,64]{3,0,2,1:T(8,128)S(1)} %maximum_divide_fusion), channel_id=1, source_target_pairs={{0,384},{128,0},{256,128},{384,256},{1,385},{129,1},{257,129},{385... | collective-permute-start | bytes 491528 | tf_op jit(solution)/shard_map/ppermute | solution.py:23
  379.9 8.5 %collective-permute-done.5 = f32[5,8,16,64]{3,0,2,1:T(8,128)S(1)} collective-permute-done((f32[5,8,16,64]{3,0,2,1:T(8,128)S(1)}, f32[5,8,16,64]{3,0,2,1:T(8,128)S(1)}, u32[]{:S(2)}, u32[]{:S(2)}) %collective-permute-start.5) | collective-permute-done | bytes 163872 | tf_op jit(solution)/shard_map/ppermute | solution.py:21
  391.9 11.2 %collective-permute-done.6 = f32[5,8,16,64]{3,0,2,1:T(8,128)} collective-permute-done((f32[5,8,16,64]{3,0,2,1:T(8,128)S(1)}, f32[5,8,16,64]{3,0,2,1:T(8,128)}, u32[]{:S(2)}, u32[]{:S(2)}) %collective-permute-start.6) | collective-permute-done | bytes 163872 | tf_op jit(solution)/shard_map/ppermute | solution.py:21
  403.1 3.2 concatenate.65
  (645 shorter events, 158.6 us)
Async XLA Ops:
  7.2 354.7 %reduce-scatter.4.cloned.1.call-start = ((), (), s32[]{:S(2)}) async-start(), calls=%async_computation.1 | async-start | bytes 819200
  7.2 24.0 %copy-start.7 = (f32[5,8,16,256]{3,2,1,0:T(8,128)S(1)}, f32[5,8,16,256]{3,2,1,0:T(8,128)}, u32[]{:S(2)}) copy-start(f32[5,8,16,256]{3,2,1,0:T(8,128)} %param.11) | copy-start | bytes 1966084
  8.7 21.3 %collective-permute-start.3 = (f32[7,8,8,256]{3,2,1,0:T(8,128)S(1)}, f32[7,8,8,256]{3,2,1,0:T(8,128)S(1)}, u32[]{:S(2)}, u32[]{:S(2)}) collective-permute-start(f32[7,8,8,256]{3,2,1,0:T(8,128)S(1)} %get-tuple-element.112), channel_id=1, source_target_pairs={{0,8},{8,16},{16,24},{24,32},{32,40},{40,48},{48,56},{56,64},{64,7... | collective-permute-start | bytes 1376264 | tf_op jit(solution)/shard_map/ppermute | solution.py:36
  13.0 18.2 %collective-permute-start.4 = (f32[7,8,8,256]{3,2,1,0:T(8,128)S(1)}, f32[7,8,8,256]{3,2,1,0:T(8,128)}, u32[]{:S(2)}, u32[]{:S(2)}) collective-permute-start(f32[7,8,8,256]{3,2,1,0:T(8,128)S(1)} %get-tuple-element.113), channel_id=1, source_target_pairs={{8,0},{16,8},{24,16},{32,24},{40,32},{48,40},{56,48},{64,56},{72,6... | collective-permute-start | bytes 1376264 | tf_op jit(solution)/shard_map/ppermute | solution.py:38
  37.5 252.0 %copy-start.15 = (f32[8]{0:T(128)S(1)}, f32[8]{0:T(128)}, u32[]{:S(2)}) copy-start(f32[8]{0:T(128)} %param.13) | copy-start | bytes 100
  38.6 13.2 %collective-permute-start = (f32[8,2,8,256]{3,2,0,1:T(8,128)}, f32[8,2,8,256]{3,2,0,1:T(8,128)}, u32[]{:S(2)}, u32[]{:S(2)}) collective-permute-start(f32[8,2,8,256]{3,2,0,1:T(8,128)} %get-tuple-element.207), channel_id=1, source_target_pairs={{0,8},{8,16},{16,24},{24,32},{32,40},{40,48},{48,56},{56,64},{64,7... | collective-permute-start | bytes 393224 | tf_op jit(solution)/shard_map/while/body/eval_jaxpr/ppermute | solution.py:36
  40.5 13.2 %collective-permute-start.1 = (f32[8,2,8,256]{3,2,0,1:T(8,128)}, f32[8,2,8,256]{3,2,0,1:T(8,128)}, u32[]{:S(2)}, u32[]{:S(2)}) collective-permute-start(f32[8,2,8,256]{3,2,0,1:T(8,128)} %get-tuple-element.208), channel_id=1, source_target_pairs={{8,0},{16,8},{24,16},{32,24},{40,32},{48,40},{56,48},{64,56},{72,6... | collective-permute-start | bytes 393224 | tf_op jit(solution)/shard_map/while/body/eval_jaxpr/ppermute | solution.py:38
  61.9 2.4 collective-permute-start.2
  65.1 12.6 %collective-permute-start = (f32[8,2,8,256]{3,2,0,1:T(8,128)}, f32[8,2,8,256]{3,2,0,1:T(8,128)}, u32[]{:S(2)}, u32[]{:S(2)}) collective-permute-start(f32[8,2,8,256]{3,2,0,1:T(8,128)} %get-tuple-element.207), channel_id=1, source_target_pairs={{0,8},{8,16},{16,24},{24,32},{32,40},{40,48},{48,56},{56,64},{64,7... | collective-permute-start | bytes 393224 | tf_op jit(solution)/shard_map/while/body/eval_jaxpr/ppermute | solution.py:36
  67.1 12.6 %collective-permute-start.1 = (f32[8,2,8,256]{3,2,0,1:T(8,128)}, f32[8,2,8,256]{3,2,0,1:T(8,128)}, u32[]{:S(2)}, u32[]{:S(2)}) collective-permute-start(f32[8,2,8,256]{3,2,0,1:T(8,128)} %get-tuple-element.208), channel_id=1, source_target_pairs={{8,0},{16,8},{24,16},{32,24},{40,32},{48,40},{56,48},{64,56},{72,6... | collective-permute-start | bytes 393224 | tf_op jit(solution)/shard_map/while/body/eval_jaxpr/ppermute | solution.py:38
  87.9 8.0 %collective-permute-start.2 = (f32[8,2,16,256]{3,2,0,1:T(8,128)S(1)}, f32[8,2,16,256]{3,2,0,1:T(8,128)S(1)}, u32[]{:S(2)}, u32[]{:S(2)}) collective-permute-start(f32[8,2,16,256]{3,2,0,1:T(8,128)S(1)} %get-tuple-element.242), channel_id=1, source_target_pairs={{0,1},{1,2},{2,3},{3,4},{4,5},{5,6},{6,7},{8,9},{9,10},{10,11},{11... | collective-permute-start | bytes 786440 | tf_op jit(solution)/shard_map/while/body/eval_jaxpr/ppermute | solution.py:48
  96.6 12.6 %collective-permute-start = (f32[8,2,8,256]{3,2,0,1:T(8,128)}, f32[8,2,8,256]{3,2,0,1:T(8,128)}, u32[]{:S(2)}, u32[]{:S(2)}) collective-permute-start(f32[8,2,8,256]{3,2,0,1:T(8,128)} %get-tuple-element.207), channel_id=1, source_target_pairs={{0,8},{8,16},{16,24},{24,32},{32,40},{40,48},{48,56},{56,64},{64,7... | collective-permute-start | bytes 393224 | tf_op jit(solution)/shard_map/while/body/eval_jaxpr/ppermute | solution.py:36
  98.6 12.6 %collective-permute-start.1 = (f32[8,2,8,256]{3,2,0,1:T(8,128)}, f32[8,2,8,256]{3,2,0,1:T(8,128)}, u32[]{:S(2)}, u32[]{:S(2)}) collective-permute-start(f32[8,2,8,256]{3,2,0,1:T(8,128)} %get-tuple-element.208), channel_id=1, source_target_pairs={{8,0},{16,8},{24,16},{32,24},{40,32},{48,40},{56,48},{64,56},{72,6... | collective-permute-start | bytes 393224 | tf_op jit(solution)/shard_map/while/body/eval_jaxpr/ppermute | solution.py:38
  119.4 8.7 %collective-permute-start.2 = (f32[8,2,16,256]{3,2,0,1:T(8,128)S(1)}, f32[8,2,16,256]{3,2,0,1:T(8,128)S(1)}, u32[]{:S(2)}, u32[]{:S(2)}) collective-permute-start(f32[8,2,16,256]{3,2,0,1:T(8,128)S(1)} %get-tuple-element.242), channel_id=1, source_target_pairs={{0,1},{1,2},{2,3},{3,4},{4,5},{5,6},{6,7},{8,9},{9,10},{10,11},{11... | collective-permute-start | bytes 786440 | tf_op jit(solution)/shard_map/while/body/eval_jaxpr/ppermute | solution.py:48
  128.8 12.6 %collective-permute-start = (f32[8,2,8,256]{3,2,0,1:T(8,128)}, f32[8,2,8,256]{3,2,0,1:T(8,128)}, u32[]{:S(2)}, u32[]{:S(2)}) collective-permute-start(f32[8,2,8,256]{3,2,0,1:T(8,128)} %get-tuple-element.207), channel_id=1, source_target_pairs={{0,8},{8,16},{16,24},{24,32},{32,40},{40,48},{48,56},{56,64},{64,7... | collective-permute-start | bytes 393224 | tf_op jit(solution)/shard_map/while/body/eval_jaxpr/ppermute | solution.py:36
  130.7 12.6 %collective-permute-start.1 = (f32[8,2,8,256]{3,2,0,1:T(8,128)}, f32[8,2,8,256]{3,2,0,1:T(8,128)}, u32[]{:S(2)}, u32[]{:S(2)}) collective-permute-start(f32[8,2,8,256]{3,2,0,1:T(8,128)} %get-tuple-element.208), channel_id=1, source_target_pairs={{8,0},{16,8},{24,16},{32,24},{40,32},{48,40},{56,48},{64,56},{72,6... | collective-permute-start | bytes 393224 | tf_op jit(solution)/shard_map/while/body/eval_jaxpr/ppermute | solution.py:38
  151.6 8.7 %collective-permute-start.2 = (f32[8,2,16,256]{3,2,0,1:T(8,128)S(1)}, f32[8,2,16,256]{3,2,0,1:T(8,128)S(1)}, u32[]{:S(2)}, u32[]{:S(2)}) collective-permute-start(f32[8,2,16,256]{3,2,0,1:T(8,128)S(1)} %get-tuple-element.242), channel_id=1, source_target_pairs={{0,1},{1,2},{2,3},{3,4},{4,5},{5,6},{6,7},{8,9},{9,10},{10,11},{11... | collective-permute-start | bytes 786440 | tf_op jit(solution)/shard_map/while/body/eval_jaxpr/ppermute | solution.py:48
  161.1 12.6 %collective-permute-start = (f32[8,2,8,256]{3,2,0,1:T(8,128)}, f32[8,2,8,256]{3,2,0,1:T(8,128)}, u32[]{:S(2)}, u32[]{:S(2)}) collective-permute-start(f32[8,2,8,256]{3,2,0,1:T(8,128)} %get-tuple-element.207), channel_id=1, source_target_pairs={{0,8},{8,16},{16,24},{24,32},{32,40},{40,48},{48,56},{56,64},{64,7... | collective-permute-start | bytes 393224 | tf_op jit(solution)/shard_map/while/body/eval_jaxpr/ppermute | solution.py:36
  163.0 12.6 %collective-permute-start.1 = (f32[8,2,8,256]{3,2,0,1:T(8,128)}, f32[8,2,8,256]{3,2,0,1:T(8,128)}, u32[]{:S(2)}, u32[]{:S(2)}) collective-permute-start(f32[8,2,8,256]{3,2,0,1:T(8,128)} %get-tuple-element.208), channel_id=1, source_target_pairs={{8,0},{16,8},{24,16},{32,24},{40,32},{48,40},{56,48},{64,56},{72,6... | collective-permute-start | bytes 393224 | tf_op jit(solution)/shard_map/while/body/eval_jaxpr/ppermute | solution.py:38
  183.8 8.7 %collective-permute-start.2 = (f32[8,2,16,256]{3,2,0,1:T(8,128)S(1)}, f32[8,2,16,256]{3,2,0,1:T(8,128)S(1)}, u32[]{:S(2)}, u32[]{:S(2)}) collective-permute-start(f32[8,2,16,256]{3,2,0,1:T(8,128)S(1)} %get-tuple-element.242), channel_id=1, source_target_pairs={{0,1},{1,2},{2,3},{3,4},{4,5},{5,6},{6,7},{8,9},{9,10},{10,11},{11... | collective-permute-start | bytes 786440 | tf_op jit(solution)/shard_map/while/body/eval_jaxpr/ppermute | solution.py:48
  193.3 12.6 %collective-permute-start = (f32[8,2,8,256]{3,2,0,1:T(8,128)}, f32[8,2,8,256]{3,2,0,1:T(8,128)}, u32[]{:S(2)}, u32[]{:S(2)}) collective-permute-start(f32[8,2,8,256]{3,2,0,1:T(8,128)} %get-tuple-element.207), channel_id=1, source_target_pairs={{0,8},{8,16},{16,24},{24,32},{32,40},{40,48},{48,56},{56,64},{64,7... | collective-permute-start | bytes 393224 | tf_op jit(solution)/shard_map/while/body/eval_jaxpr/ppermute | solution.py:36
  195.2 12.6 %collective-permute-start.1 = (f32[8,2,8,256]{3,2,0,1:T(8,128)}, f32[8,2,8,256]{3,2,0,1:T(8,128)}, u32[]{:S(2)}, u32[]{:S(2)}) collective-permute-start(f32[8,2,8,256]{3,2,0,1:T(8,128)} %get-tuple-element.208), channel_id=1, source_target_pairs={{8,0},{16,8},{24,16},{32,24},{40,32},{48,40},{56,48},{64,56},{72,6... | collective-permute-start | bytes 393224 | tf_op jit(solution)/shard_map/while/body/eval_jaxpr/ppermute | solution.py:38
  216.1 8.7 %collective-permute-start.2 = (f32[8,2,16,256]{3,2,0,1:T(8,128)S(1)}, f32[8,2,16,256]{3,2,0,1:T(8,128)S(1)}, u32[]{:S(2)}, u32[]{:S(2)}) collective-permute-start(f32[8,2,16,256]{3,2,0,1:T(8,128)S(1)} %get-tuple-element.242), channel_id=1, source_target_pairs={{0,1},{1,2},{2,3},{3,4},{4,5},{5,6},{6,7},{8,9},{9,10},{10,11},{11... | collective-permute-start | bytes 786440 | tf_op jit(solution)/shard_map/while/body/eval_jaxpr/ppermute | solution.py:48
  225.6 12.6 %collective-permute-start = (f32[8,2,8,256]{3,2,0,1:T(8,128)}, f32[8,2,8,256]{3,2,0,1:T(8,128)}, u32[]{:S(2)}, u32[]{:S(2)}) collective-permute-start(f32[8,2,8,256]{3,2,0,1:T(8,128)} %get-tuple-element.207), channel_id=1, source_target_pairs={{0,8},{8,16},{16,24},{24,32},{32,40},{40,48},{48,56},{56,64},{64,7... | collective-permute-start | bytes 393224 | tf_op jit(solution)/shard_map/while/body/eval_jaxpr/ppermute | solution.py:36
  227.5 12.6 %collective-permute-start.1 = (f32[8,2,8,256]{3,2,0,1:T(8,128)}, f32[8,2,8,256]{3,2,0,1:T(8,128)}, u32[]{:S(2)}, u32[]{:S(2)}) collective-permute-start(f32[8,2,8,256]{3,2,0,1:T(8,128)} %get-tuple-element.208), channel_id=1, source_target_pairs={{8,0},{16,8},{24,16},{32,24},{40,32},{48,40},{56,48},{64,56},{72,6... | collective-permute-start | bytes 393224 | tf_op jit(solution)/shard_map/while/body/eval_jaxpr/ppermute | solution.py:38
  248.3 8.7 %collective-permute-start.2 = (f32[8,2,16,256]{3,2,0,1:T(8,128)S(1)}, f32[8,2,16,256]{3,2,0,1:T(8,128)S(1)}, u32[]{:S(2)}, u32[]{:S(2)}) collective-permute-start(f32[8,2,16,256]{3,2,0,1:T(8,128)S(1)} %get-tuple-element.242), channel_id=1, source_target_pairs={{0,1},{1,2},{2,3},{3,4},{4,5},{5,6},{6,7},{8,9},{9,10},{10,11},{11... | collective-permute-start | bytes 786440 | tf_op jit(solution)/shard_map/while/body/eval_jaxpr/ppermute | solution.py:48
  257.8 12.6 %collective-permute-start = (f32[8,2,8,256]{3,2,0,1:T(8,128)}, f32[8,2,8,256]{3,2,0,1:T(8,128)}, u32[]{:S(2)}, u32[]{:S(2)}) collective-permute-start(f32[8,2,8,256]{3,2,0,1:T(8,128)} %get-tuple-element.207), channel_id=1, source_target_pairs={{0,8},{8,16},{16,24},{24,32},{32,40},{40,48},{48,56},{56,64},{64,7... | collective-permute-start | bytes 393224 | tf_op jit(solution)/shard_map/while/body/eval_jaxpr/ppermute | solution.py:36
  259.7 12.6 %collective-permute-start.1 = (f32[8,2,8,256]{3,2,0,1:T(8,128)}, f32[8,2,8,256]{3,2,0,1:T(8,128)}, u32[]{:S(2)}, u32[]{:S(2)}) collective-permute-start(f32[8,2,8,256]{3,2,0,1:T(8,128)} %get-tuple-element.208), channel_id=1, source_target_pairs={{8,0},{16,8},{24,16},{32,24},{40,32},{48,40},{56,48},{64,56},{72,6... | collective-permute-start | bytes 393224 | tf_op jit(solution)/shard_map/while/body/eval_jaxpr/ppermute | solution.py:38
  280.6 9.0 %collective-permute-start.2 = (f32[8,2,16,256]{3,2,0,1:T(8,128)S(1)}, f32[8,2,16,256]{3,2,0,1:T(8,128)S(1)}, u32[]{:S(2)}, u32[]{:S(2)}) collective-permute-start(f32[8,2,16,256]{3,2,0,1:T(8,128)S(1)} %get-tuple-element.242), channel_id=1, source_target_pairs={{0,1},{1,2},{2,3},{3,4},{4,5},{5,6},{6,7},{8,9},{9,10},{10,11},{11... | collective-permute-start | bytes 786440 | tf_op jit(solution)/shard_map/while/body/eval_jaxpr/ppermute | solution.py:48
  372.8 15.6 %collective-permute-start.5 = (f32[5,8,16,64]{3,0,2,1:T(8,128)S(1)}, f32[5,8,16,64]{3,0,2,1:T(8,128)S(1)}, u32[]{:S(2)}, u32[]{:S(2)}) collective-permute-start(f32[5,8,16,64]{3,0,2,1:T(8,128)S(1)} %maximum_divide_fusion), channel_id=1, source_target_pairs={{0,128},{128,256},{256,384},{384,0},{1,129},{129,257},{257,385},{3... | collective-permute-start | bytes 491528 | tf_op jit(solution)/shard_map/ppermute | solution.py:21
  374.8 16.3 %collective-permute-start.7 = (f32[5,8,16,64]{3,0,2,1:T(8,128)S(1)}, f32[5,8,16,64]{3,0,2,1:T(8,128)S(1)}, u32[]{:S(2)}, u32[]{:S(2)}) collective-permute-start(f32[5,8,16,64]{3,0,2,1:T(8,128)S(1)} %maximum_divide_fusion), channel_id=1, source_target_pairs={{0,384},{128,0},{256,128},{384,256},{1,385},{129,1},{257,129},{385... | collective-permute-start | bytes 491528 | tf_op jit(solution)/shard_map/ppermute | solution.py:23
  388.4 14.7 %collective-permute-start.6 = (f32[5,8,16,64]{3,0,2,1:T(8,128)S(1)}, f32[5,8,16,64]{3,0,2,1:T(8,128)}, u32[]{:S(2)}, u32[]{:S(2)}) collective-permute-start(f32[5,8,16,64]{3,0,2,1:T(8,128)S(1)} %collective-permute-done.5), channel_id=1, source_target_pairs={{0,128},{128,256},{256,384},{384,0},{1,129},{129,257},{257,385},{3... | collective-permute-start | bytes 491528 | tf_op jit(solution)/shard_map/ppermute | solution.py:21
  (71 other events, 308.3 us)
Sparse Core Ops, SparseCore 0:
  318.1 43.6 reduce-scatter.3
